TPU v7x, 32 devices: a whole 2x2x4 slice. The times are simulated.
32 devices in a mesh: groups: 2 (over y), tmpl: 4 (over z), chan: 2 (over x), tm: 2 (over core).
Axes of the slice: x: 2, y: 2, z: 4, core: 2. Of those that a mesh axis runs over, the one named last changes fastest.
Arguments:
- samples: bfloat16 [1792, 3584], P(('tmpl', 'chan'), ('groups', 'tm')), parts along dimension 1, may hold values from -6 to 6
- tail: bfloat16 [1792, 1792], P(('tmpl', 'chan'), 'groups'), parts along dimension 1, may hold values from -6 to 6
- templates: bfloat16 [128, 8, 640], P('tmpl', 'chan'), may hold values from -6 to 6
- channels: int32 [128, 8], P('tmpl', 'chan'), may hold values from 0 to 1791
- moveouts: int32 [128, 8], P('tmpl', 'chan'), may hold values from 0 to 256
- live: int32 [128], P('tmpl'), may hold values from 4 to 8
Outputs:
- detection: float32 [128, 3584], P(('tmpl', 'chan'), ('groups', 'tm')), parts along dimension 1
There are 2 independent parts, one for each index of `groups`. A program takes and returns all parts, laid end to end along the dimension named above; an argument that names none is the same for every part. Nothing has to cross between parts.
All inputs are finite; a program needn't handle non-finite values.
Results may differ from a plain program's by a relative error of at most 0.0003.
Values may be sent and summed in bfloat16 or wider, within the bound.
No kernel may reach another device: no remote copies, remote signals or barrier semaphores. Data moves between devices by JAX's collectives and lax.ppermute only.
A program may use at most 64 MiB of HBM per device.

v0:
```python
import jax
import jax.numpy as jnp
from jax import lax
from jax.sharding import PartitionSpec as P

EPS = 1e-06


def shifted(block, axis, distance):
    devices = range(lax.axis_size(axis))
    route = [(i - distance, i) for i in devices if i - distance in devices]
    return lax.ppermute(block, axis, route)


def depthwise(signal, kernel):
    output = lax.conv_general_dilated(
        signal[None],
        kernel[:, None, :],
        (1,),
        "VALID",
        dimension_numbers=("NCH", "OIH", "NCH"),
        feature_group_count=signal.shape[0],
        precision=None,
        preferred_element_type=jnp.float32,
    )
    return output[0]


def shifted_rows(window, chan_ids, offsets, length):
    picked = jnp.take(window, chan_ids, axis=0)

    def one_row(row_data, offset):
        return lax.dynamic_slice_in_dim(row_data, offset, length)

    return jax.vmap(one_row)(picked, offsets)


def running_energy(squares, length):
    totals = jnp.cumsum(squares, axis=1)
    totals = jnp.concatenate([jnp.zeros((squares.shape[0], 1), jnp.float32), totals], axis=1)
    return totals[:, length:] - totals[:, : totals.shape[1] - length]


def body(samples, tail, templates, channels, moveouts, live):
    block = samples.shape[1]
    length = templates.shape[2]
    per_dev = templates.shape[0]
    per_slot = templates.shape[1]
    is_last = lax.axis_index("tm") == lax.axis_size("tm") - 1
    gathered, tail_all = (
        lax.all_gather(samples, ("tmpl", "chan"), axis=0, tiled=True),
        lax.all_gather(tail, ("tmpl", "chan"), axis=0, tiled=True),
    )
    following = shifted(gathered, "tm", -1)
    rim_all = jnp.where(is_last, tail_all, following)
    window = jnp.concatenate([gathered, rim_all], axis=1)
    slots = per_dev * per_slot
    chan_ids = channels.reshape(slots)
    offsets = moveouts.reshape(slots)
    waveform = templates.reshape(slots, length)
    slot_data = shifted_rows(window, chan_ids, offsets, block + length)
    correlation = depthwise(slot_data, waveform)[:, :block]
    squares = slot_data.astype(jnp.float32) ** 2
    energy = running_energy(squares, length)[:, :block]
    tnorm = jnp.sqrt(jnp.sum(waveform.astype(jnp.float32) ** 2, axis=-1) + EPS)
    ncc = correlation / (tnorm[:, None] * jnp.sqrt(energy + EPS))
    slot_index = lax.axis_index("chan") * per_slot + jnp.arange(per_slot)
    used_f = live.astype(jnp.float32)
    weight = jnp.where(
        slot_index[None, :] < live[:, None],
        jnp.sqrt(jnp.float32(length) / used_f)[:, None],
        jnp.float32(0.0),
    )
    partial_value = jnp.sum(weight[:, :, None] * ncc.reshape(per_dev, per_slot, block), axis=1)
    return lax.psum_scatter(partial_value, "chan", scatter_dimension=0, tiled=True)


def solution(mesh):
    in_specs = (
        P(("tmpl", "chan"), ("groups", "tm")),
        P(("tmpl", "chan"), "groups"),
        P("tmpl", "chan", None),
        P("tmpl", "chan"),
        P("tmpl", "chan"),
        P("tmpl"),
    )
    out_specs = P(("tmpl", "chan"), ("groups", "tm"))
    return jax.shard_map(body, mesh=mesh, in_specs=in_specs, out_specs=out_specs, check_vma=False)
```

profile of v0, /device:TPU:0, one launch (start us, length us, event | category | flops | bytes accessed | tf_op | source)
XLA Modules:
  0.0 499.8 jit_solution(5744314067343996593)
XLA Ops:
  8.1 64.9 %all-gather.3.cloned.1.call-done = bf16[1792,896]{1,0:T(8,128)(2,1)} async-done(((bf16[224,896]{1,0:T(8,128)(2,1)}), bf16[1792,896]{1,0:T(8,128)(2,1)}) %all-gather.3.cloned.1.call-update) | async-done | bytes 3211280 | tf_op jit(solution)/shard_map/all_gather | solution.py:51
  82.1 52.4 %all-gather.5.cloned.1.call-done = bf16[1792,896]{1,0:T(8,128)(2,1)} async-done(((bf16[224,896]{1,0:T(8,128)(2,1)}), bf16[1792,896]{1,0:T(8,128)(2,1)}) %all-gather.5.cloned.1.call-update) | async-done | bytes 3211280 | tf_op jit(solution)/shard_map/all_gather | solution.py:52
  134.5 2.3 broadcast_select_fusion
  136.8 3.1 pad_maximum_fusion
  139.9 5.2 %gather_fusion = bf16[128,1792]{1,0:T(8,128)(2,1)S(1)} fusion(bf16[1792,1792]{1,0:T(8,128)(2,1)} %pad_maximum_fusion, s32[1024]{0:T(1024)} %pad_clamp_fusion), kind=kCustom, calls=%fused_computation | custom fusion | bytes 918016 | tf_op jit(solution)/shard_map/jit(_take)/gather | solution.py:30
  145.2 264.2 %while.1 = (s32[]{:T(128)}, bf16[128,1792]{1,0:T(8,128)(2,1)S(1)}, s32[128,2]{0,1:T(2,128)S(1)}, bf16[128,1536]{1,0:T(8,128)(2,1)S(1)}, s32[]{:T(128)}, /*index=5*/s32[]{:T(128)}) while((s32[]{:T(128)}, bf16[128,1792]{1,0:T(8,128)(2,1)S(1)}, s32[128,2]{0,1:T(2,128)S(1)}, bf16[128,1536]{1,0:T(8,128)(2,1)S(1)}, s32[]{:T(128)}, /*index=5*/s32[]{:T(128)}) %tuple.30), condition=%wide.while_cond, body=%wide.while_body.sunk | while | flops 2 | bytes 12401 | solution.py:33
  145.9 1.3 dynamic-slice.7
  147.9 1.3 dynamic-slice.7
  154.1 1.3 dynamic-slice.7
  156.2 1.3 dynamic-slice.7
  158.2 1.3 dynamic-slice.7
  162.4 1.3 dynamic-slice.7
  164.4 1.3 dynamic-slice.7
  166.5 1.3 dynamic-slice.7
  172.7 1.3 dynamic-slice.7
  174.7 1.3 dynamic-slice.7
  176.8 1.3 dynamic-slice.7
  183.0 1.3 dynamic-slice.7
  185.1 1.3 dynamic-slice.7
  187.1 1.3 dynamic-slice.7
  193.3 1.3 dynamic-slice.7
  195.4 1.3 dynamic-slice.7
  197.4 1.3 dynamic-slice.7
  201.6 1.3 dynamic-slice.7
  203.6 1.3 dynamic-slice.7
  205.7 1.3 dynamic-slice.7
  211.9 1.3 dynamic-slice.7
  214.0 1.3 dynamic-slice.7
  216.0 1.3 dynamic-slice.7
  222.2 1.3 dynamic-slice.7
  224.3 1.3 dynamic-slice.7
  226.3 1.3 dynamic-slice.7
  232.5 1.3 dynamic-slice.7
  234.6 1.3 dynamic-slice.7
  236.7 1.3 dynamic-slice.7
  240.8 1.3 dynamic-slice.7
  242.8 1.3 dynamic-slice.7
  244.9 1.3 dynamic-slice.7
  251.1 1.3 dynamic-slice.7
  253.2 1.3 dynamic-slice.7
  255.2 1.3 dynamic-slice.7
  261.4 1.3 dynamic-slice.7
  263.5 1.3 dynamic-slice.7
  265.5 1.3 dynamic-slice.7
  271.7 1.3 dynamic-slice.7
  273.8 1.3 dynamic-slice.7
  411.2 71.3 %fusion.9 = f32[1,128,897]{1,0,2:T(1,128)S(1)} fusion(bf16[1,128,1536]{1,0,2:T(2,128)(2,1)S(1)} %copy.17, bf16[128,1,640]{0,1,2:T(2,128)(2,1)S(1)} %copy.18), kind=kOutput, calls=%fused_computation.32 | convolution fusion | flops 146964480 | bytes 1016320 | tf_op jit(solution)/shard_map/conv_general_dilated | solution.py:16
  484.1 9.1 %reduce-scatter.2.cloned.1.call-done = f32[16,896]{1,0:T(8,128)} async-done(((f32[32,896]{1,0:T(8,128)}), f32[16,896]{1,0:T(8,128)}) %reduce-scatter.2.cloned.1.call-update) | async-done | bytes 57360 | tf_op jit(solution)/shard_map/reduce_scatter | solution.py:75
  (525 shorter events, 221.4 us)
Async XLA Ops:
  6.5 66.4 %all-gather.3.cloned.1.call-start = ((), (), s32[]{:S(2)}) async-start(), calls=%async_computation.1 | async-start | bytes 3612672 | tf_op jit(solution)/shard_map/all_gather | solution.py:51
  7.3 127.2 %all-gather.5.cloned.1.call-start = ((), (), s32[]{:S(2)}) async-start(), calls=%async_computation.2 | async-start | bytes 3612672 | tf_op jit(solution)/shard_map/all_gather | solution.py:52
  8.0 485.2 %reduce-scatter.2.cloned.1.call-start = ((), (), s32[]{:S(2)}) async-start(), calls=%async_computation.3 | async-start | bytes 172032 | tf_op jit(solution)/shard_map/reduce_scatter | solution.py:75
  72.9 61.6 %collective-permute-start = (bf16[1792,896]{1,0:T(8,128)(2,1)}, bf16[1792,896]{1,0:T(8,128)(2,1)}, u32[]{:S(2)}, u32[]{:S(2)}) collective-permute-start(bf16[1792,896]{1,0:T(8,128)(2,1)} %all-gather.3.cloned.1.call-done), channel_id=1, source_target_pairs={{1,0},{3,2},{5,4},{7,6},{9,8},{11,10},{13,12},{15,14},{17,16},{19,... | collective-permute-start | bytes 9633800 | tf_op jit(solution)/shard_map/ppermute | solution.py:12
  82.1 54.7 %copy-start = (bf16[1792,896]{1,0:T(8,128)(2,1)S(1)}, bf16[1792,896]{1,0:T(8,128)(2,1)}, u32[]{:S(2)}) copy-start(bf16[1792,896]{1,0:T(8,128)(2,1)} %all-gather.3.cloned.1.call-done) | copy-start | bytes 9633796
  139.9 5.2 %copy-start.4 = (pred[128]{0:T(512)(128)(4,1)S(1)}, pred[128]{0:T(512)(128)(4,1)}, u32[]{:S(2)}) copy-start(pred[128]{0:T(512)(128)(4,1)} %compare_and_fusion) | copy-start | bytes 388
  139.9 5.3 %copy-start.1 = (bf16[128,1536]{1,0:T(8,128)(2,1)S(1)}, bf16[128,1536]{1,0:T(8,128)(2,1)}, u32[]{:S(2)}) copy-start(bf16[128,1536]{1,0:T(8,128)(2,1)} %custom-call.2) | copy-start | bytes 1179652
  139.9 5.3 %copy-start.2 = (s32[128,2]{0,1:T(2,128)S(1)}, s32[128,2]{0,1:T(2,128)}, u32[]{:S(2)}) copy-start(s32[128,2]{0,1:T(2,128)} %pad_add_fusion) | copy-start | bytes 3076
  411.2 71.4 %copy-start.3 = (f32[128]{0:T(128)S(1)}, f32[128]{0:T(128)}, u32[]{:S(2)}) copy-start(f32[128]{0:T(128)} %sqrt.18) | copy-start | bytes 1540
Sparse Core Ops, SparseCore 0:
  9.5 63.3 all-gather.2
  75.1 59.3 all-gather.4
  484.3 8.9 reduce-scatter.1
where the time goes:
time: 502 us; the launch traced here: 500 us
  local copies, waits for them, and re-layouts  271 us (54%)
  waiting for transfers between devices  128 us (25%)
  matrix products  71.3 us (14%)
  between operations  13.3 us (3%)
  other arithmetic  11.5 us (2%)
    gather x512, local copies, waits for them, and re-layouts  261 us
    conv_general_dilated x1, matrix products, depthwise(): lax.conv_general_dilated(signal[None], kernel[:, None, :], (1,), 'VALID',...  71.3 us
    all_gather x1, waiting for transfers between devices, body(): lax.all_gather(samples, ('tmpl', 'chan'), axis=0, tiled=True)  64.9 us
    all_gather x1, waiting for transfers between devices, body(): lax.all_gather(tail, ('tmpl', 'chan'), axis=0, tiled=True)  52.4 us
  transfers between devices with their start and end apart: 4, of which 3 were waited for; matrix products, arithmetic and copies ran while one was open for 2% of the time, Pallas kernels for 0%

commit v1 on v0

v1 whole, which is shorter than its diff:
```python
import jax
import jax.numpy as jnp
from jax import lax
from jax.experimental import pallas as pl
from jax.experimental.pallas import tpu as pltpu
from jax.sharding import PartitionSpec as P


EPS = 1e-06
LANES = 128
DEPTH = 16
BATCH = 16
F32 = jnp.float32
BF16 = jnp.bfloat16
GROUP = ("tmpl", "chan")


def bucket_rows(slots, buckets):
    mean = slots / buckets
    return 16 * int(-(-(mean + 4 * mean**0.5) // 16))


def spot_of(i):
    return LANES // DEPTH - 1 - i % (LANES // DEPTH)


def iota(shape, axis):
    return lax.broadcasted_iota(jnp.int32, shape, axis)


def across(a, b):
    return lax.dot_general(a, b, (((1,), (1,)), ((), ())), preferred_element_type=F32)


def here():
    return lax.axis_index("tmpl") * lax.axis_size("chan") + lax.axis_index("chan")


def pack_kernel(groups, depth, owned, turn, templates_in, channels_in, moveouts_in, live_in, *rest):
    outs = rest[: len(groups)]
    templates, channels, moveouts, live, lined, sems = rest[len(groups) :]
    copies = [
        pltpu.make_async_copy(a, b, sems.at[i])
        for i, (a, b) in enumerate(
            ((channels_in, channels), (moveouts_in, moveouts), (live_in, live), (templates_in, templates))
        )
    ]
    for copy in copies:
        copy.start()
    first = F32(0) if turn is None else (turn[0] * depth).astype(F32)
    per_slot, rows = channels.shape
    slots, length = lined.shape
    for copy in copies[:3]:
        copy.wait()
    used = jnp.broadcast_to(live[...], (per_slot, rows))
    position = iota((per_slot, rows), 0) + lax.axis_index("chan") * per_slot
    owner = channels[...] // owned
    tag = jnp.where(position < used, owner, -1)
    widen = jnp.where(iota((rows, slots), 1) // per_slot == iota((rows, slots), 0), 1.0, 0.0).astype(BF16)
    own_row = iota((per_slot, slots), 1) % per_slot == iota((per_slot, slots), 0)

    def line(values):
        wide = jnp.dot(values.astype(F32).astype(BF16), widen, preferred_element_type=F32)
        return jnp.sum(jnp.where(own_row, wide, 0.0), axis=0, keepdims=True)

    tag_line = line(tag)
    tag_row = jnp.broadcast_to(tag_line, (slots, slots))
    same = (tag_row.T == tag_row) & (iota((slots, slots), 0) < iota((slots, slots), 1))
    rank = jnp.sum(jnp.where(same, 1.0, 0.0), axis=0, keepdims=True)
    rounds = jnp.ceil((jnp.max(jnp.where(tag_line >= 0, rank, -1.0)) + 1.0) / depth)
    known = [channels[...] - owner * owned, moveouts[...], iota((per_slot, rows), 1), used]
    facts = jnp.zeros((LANES, slots), F32)
    which = iota((LANES, slots), 0)
    for at, fact in enumerate(known):
        facts = jnp.where(which == at, jnp.broadcast_to(line(fact), (LANES, slots)), facts)
    facts = facts.astype(BF16)
    copies[3].wait()
    for n in range(rows):
        lined[per_slot * n : per_slot * (n + 1), :] = templates[n].astype(F32)
    flip_row, flip_lane = iota((LANES, LANES), 0), iota((LANES, LANES), 1)
    mirrored = flip_row // DEPTH * DEPTH + DEPTH - 1 - flip_row % DEPTH
    flip = jnp.where(flip_lane == mirrored, 1.0, 0.0).astype(BF16)
    tiles = [
        jnp.dot(lined[:, LANES * q : LANES * (q + 1)].astype(BF16), flip, preferred_element_type=F32).astype(BF16)
        for q in range(length // LANES)
    ]
    place = lax.axis_index("tmpl").astype(F32)
    for out, owners in zip(outs, groups, strict=True):
        blocks, told = [], []
        for to in owners:
            fits = (tag_line == to.astype(F32)) & (tag_line >= 0) & (rank - first == iota((depth, slots), 0).astype(F32))
            block = jnp.where(fits, 1.0, 0.0)
            count = jnp.sum(block)
            lane = iota((depth, LANES), 1)
            extra = jnp.where(lane == 4, count, jnp.where(lane == 5, rounds, jnp.where(lane == 6, place, 0.0)))
            blocks.append(block.astype(BF16))
            told.append(across(block.astype(BF16), facts) + extra)
        chosen = jnp.concatenate(blocks, axis=0)
        for q, tile in enumerate(tiles):
            out[:, LANES * q : LANES * (q + 1)] = jnp.dot(chosen, tile, preferred_element_type=F32).astype(BF16)
        out[:, length:] = jnp.concatenate(told, axis=0).astype(BF16)


def pack(turn, templates, channels, moveouts, live, sizes, targets, depth, owned):
    rows, per_slot, length = templates.shape
    slots = rows * per_slot

    def kernel(*refs):
        turns, refs = (refs[0], refs[1:]) if turn is not None else (None, refs)
        pack_kernel(targets(), depth, owned, turns, *refs)

    smem = [] if turn is None else [pl.BlockSpec(memory_space=pltpu.SMEM)]
    args = (templates, channels.T, moveouts.T, live[None, :])
    return pl.pallas_call(
        kernel,
        out_shape=[jax.ShapeDtypeStruct((size * depth, length + LANES), BF16) for size in sizes],
        in_specs=smem + [pl.BlockSpec(memory_space=pl.ANY)] * 4,
        out_specs=[pl.BlockSpec(memory_space=pltpu.VMEM)] * len(sizes),
        scratch_shapes=[pltpu.VMEM(a.shape, a.dtype) for a in args]
        + [pltpu.VMEM((slots, length), F32), pltpu.SemaphoreType.DMA((4,))],
        compiler_params=pltpu.CompilerParams(vmem_limit_bytes=8 << 20),
        name="pack",
    )(*(() if turn is None else (turn.reshape(1),)), *args)


def match_kernel(dims, n_parcels, n_outs, *refs):
    near, after, tail = refs[:3]
    parcels = refs[3 : 3 + n_parcels]
    outs = refs[3 + n_parcels : 3 + n_parcels + n_outs]
    rounds_out, *refs = refs[3 + n_parcels + n_outs :]
    window, waves, scores, named, squares, sums, facts_v, facts, order, sem, hankel, toeplitz, group = refs
    depth, per_dev, per_owner, length, block = dims
    tiles, wave_tiles = block // LANES, length // LANES
    spread = tiles + wave_tiles
    owned = near.shape[0]
    rows = waves.shape[1]
    names = sum(out.shape[0] for out in outs)
    is_last = lax.axis_index("tm") == lax.axis_size("tm") - 1
    me = here() if n_outs > 1 else 0

    def line_of(place, n):
        name = place * per_dev + n
        return ((name // per_owner) ^ me) * per_owner + name % per_owner

    pick_fact = jnp.where(iota((8, LANES), 0) == iota((8, LANES), 1), 1.0, 0.0).astype(BF16)
    begin = 0
    for parcel in parcels:
        size = parcel.shape[0]
        known = across(pick_fact, parcel[:, length:]).astype(jnp.int32)
        shift = known[1:2, :]
        facts_v[0:1, begin : begin + size] = (shift // LANES * owned + known[0:1, :]) * LANES + shift % LANES
        facts_v[1:3, begin : begin + size] = known[4:6, :]
        begin += size
    tell = pltpu.make_async_copy(facts_v, facts, sem)
    tell.start()

    begin = 0
    for parcel in parcels:
        size = parcel.shape[0]
        for t in range(wave_tiles + 1):
            waves[t, begin : begin + size, :] = parcel[:, LANES * t : LANES * (t + 1)].astype(F32)
        begin += size
    for t in range(tiles):
        window[owned * t : owned * (t + 1), :] = near[:, LANES * t : LANES * (t + 1)].astype(F32)

    @pl.when(is_last)
    def _():
        for t in range(tiles):
            window[owned * (tiles + t) : owned * (tiles + t + 1), :] = tail[:, LANES * t : LANES * (t + 1)].astype(F32)

    @pl.when(jnp.logical_not(is_last))
    def _():
        for t in range(tiles):
            window[owned * (tiles + t) : owned * (tiles + t + 1), :] = after[:, LANES * t : LANES * (t + 1)].astype(F32)

    filled = 2 * tiles * owned
    if filled < window.shape[0]:
        window[filled:, :] = jnp.zeros((window.shape[0] - filled, LANES), F32)
    toeplitz[...] = jnp.zeros(toeplitz.shape, BF16)
    row, lane = iota(sums.shape, 0) % LANES, iota(sums.shape, 1)
    place, part = lane % LANES, lane // LANES
    keep = jnp.where(part == 0, row - place, jnp.where(part == 1, 0, place - row - 1))
    sums[...] = jnp.where(keep >= 0, 1.0, 0.0).astype(BF16)
    tell.wait()

    def list_block(b, carry):
        total, most = carry
        count = facts[1, b * depth]

        def put(eight, _):
            for i in range(8):
                at = b * depth + 8 * eight + i
                order[0, total + 8 * eight + i] = at
                order[1, total + 8 * eight + i] = facts[0, at]
            return 0

        lax.fori_loop(0, (count + 7) // 8, put, 0)
        return total + count, jnp.maximum(most, facts[2, b * depth])

    total, most = lax.fori_loop(0, rows // depth, list_block, (jnp.int32(0), jnp.int32(0)))
    rounds_out[0] = most

    per_tile = LANES // DEPTH
    lane8, sub8 = iota((8, LANES), 1), iota((8, LANES), 0)
    pick_row, pick_lane = iota((BATCH, BATCH * DEPTH), 0), iota((BATCH, BATCH * DEPTH), 1)
    pick_start = pick_row // per_tile * LANES + spot_of(pick_row) * DEPTH
    pick = jnp.where(pick_lane == pick_start + DEPTH - 1, 1.0, 0.0).astype(BF16)

    def build(step):
        last = [jnp.minimum(step * BATCH + i, total - 1) for i in range(BATCH)]
        at = [order[0, i] for i in last]
        word = [order[1, i] for i in last]
        for i in range(BATCH):
            for t in range(wave_tiles + 1):
                group[i : i + 1, LANES * t : LANES * (t + 1)] = waves[t, pl.ds(at[i], 1), :]
        for i in range(BATCH):
            within = lax.bitwise_and(word[i], LANES - 1)
            source = lax.shift_right_logical(word[i], LANES.bit_length() - 1)
            turned = [
                pltpu.roll(window[pl.ds(source + owned * t, 8, stride=0), :], LANES - within, 1)
                for t in range(spread + 2)
            ]
            ahead = lane8 + within < LANES
            aligned = [jnp.where(ahead, turned[t], turned[t + 1]) for t in range(spread + 1)]
            halves = []
            for half in range(DEPTH // 8):
                behind = DEPTH - 1 - 8 * half
                rolled = [pltpu.roll(line, LANES - behind, 1, stride=1, stride_axis=0) for line in aligned]
                inside = lane8 + behind - sub8 < LANES
                halves.append([jnp.where(inside, rolled[t], rolled[t + 1]) for t in range(spread)])
            line0 = LANES * (i // per_tile) + DEPTH * spot_of(i)
            for t in range(spread):
                both = jnp.concatenate([h[t] for h in halves], axis=0).astype(BF16)
                hankel[line0 : line0 + DEPTH, LANES * t : LANES * (t + 1)] = both
        for pair in range(BATCH // 2):
            block_tile = 2 * pair // per_tile
            for q in range(wave_tiles):
                two = []
                for i in (2 * pair, 2 * pair + 1):
                    line = waves[q, pl.ds(at[i], 8, stride=0), :]
                    turned = pltpu.roll(line, 0, 1, stride=DEPTH, stride_axis=0)
                    two.append(jnp.where(lane8 // DEPTH == spot_of(i), turned, 0.0))
                toeplitz[
                    q * BATCH * 8 + 16 * pair : q * BATCH * 8 + 16 * pair + 16,
                    LANES * block_tile : LANES * (block_tile + 1),
                ] = jnp.concatenate(two, axis=0).astype(BF16)

    def folded(stack, gap):
        odd = (sub8 // gap) % 2 == 1
        merged = []
        for a, b in zip(stack[: len(stack) // 2], stack[len(stack) // 2 :], strict=True):
            other = jnp.where(odd, a, b)
            back = pltpu.roll(other, gap, 0)
            if gap != 4:
                back = jnp.where(odd, back, pltpu.roll(other, 8 - gap, 0))
            merged.append(jnp.where(odd, b, a) + back)
        return merged

    def solve(step):
        wide = (tiles + 1) * LANES
        parts = jnp.zeros((BATCH * 8, wide), F32)
        for q in range(wave_tiles):
            parts = parts + jnp.dot(
                toeplitz[q * BATCH * 8 : (q + 1) * BATCH * 8, :],
                hankel[:, LANES * q : LANES * q + wide],
                preferred_element_type=F32,
            )
        plain = jnp.dot(pick, hankel[...], preferred_element_type=F32)
        square = plain * plain
        high = square.astype(BF16)
        low = (square - high.astype(F32)).astype(BF16)
        for t in range(spread):
            squares[BATCH * t : BATCH * (t + 1), :LANES] = high[:, LANES * t : LANES * (t + 1)]
            squares[BATCH * t : BATCH * (t + 1), LANES:] = low[:, LANES * t : LANES * (t + 1)]
        swept = jnp.dot(squares[...], sums[...], preferred_element_type=F32)

        def of_tile(t, which):
            return swept[BATCH * t : BATCH * (t + 1), LANES * which : LANES * (which + 1)]

        held = group[...]
        wave = held[:, :length]
        strength = jnp.sum(wave * wave, axis=1, keepdims=True)
        used = held[:, length + 3 : length + 4]
        valid = iota((BATCH, 1), 0) + step * BATCH < total
        spot = line_of(held[:, length + 6 : length + 7].astype(jnp.int32), held[:, length + 2 : length + 3].astype(jnp.int32))
        begin = pl.multiple_of(step * BATCH, BATCH)
        named[pl.ds(begin, BATCH), :] = jnp.where(iota((BATCH, names), 1) == spot, 1.0, 0.0)
        scale = jnp.where(valid, jnp.sqrt(length / used) / jnp.sqrt(strength + EPS), 0.0)

        sheared = []
        for i in range(BATCH):
            piece = (spot_of(i) + 8 - sub8) % 8
            own = [parts[8 * i : 8 * i + 8, LANES * t : LANES * (t + 1)] for t in range(tiles + 1)]
            stay = lane8 >= DEPTH * piece
            sheared.append(
                [
                    pltpu.roll(jnp.where(stay, own[t], own[t + 1]), 0, 1, stride=DEPTH, stride_axis=0)
                    for t in range(tiles)
                ]
            )
        for t in range(tiles):
            energy = of_tile(t, 0) + of_tile(t + wave_tiles, 2)
            for q in range(1, wave_tiles):
                energy = energy + of_tile(t + q, 1)
            weight = scale * lax.rsqrt(energy + EPS)
            for g in range(BATCH // 8):
                stack = [sheared[8 * g + i][t] for i in range(8)]
                for gap in (4, 2, 1):
                    stack = folded(stack, gap)
                straight = pltpu.roll(stack[0], DEPTH, 1, stride=DEPTH, stride_axis=0)
                result = straight * weight[8 * g : 8 * g + 8, :]
                scores[pl.ds(begin + 8 * g, 8), LANES * t : LANES * (t + 1)] = result

    def one_step(step, _):
        build(step)
        solve(step)
        return 0

    lax.fori_loop(0, (total + BATCH - 1) // BATCH, one_step, 0)
    for out in outs:
        out[...] = jnp.zeros(out.shape, F32)

    def stack_up(chunk, _):
        begin = pl.multiple_of(chunk * LANES, LANES)
        there = iota((LANES, 1), 0) + begin < total
        value = jnp.where(there, scores[pl.ds(begin, LANES), :], 0.0)
        where_to = jnp.where(there, named[pl.ds(begin, LANES), :], 0.0).astype(BF16)
        whole = jnp.zeros((names, block), F32)
        for _ in range(3):
            piece = value.astype(BF16)
            value = value - piece.astype(F32)
            whole = whole + lax.dot_general(where_to, piece, (((0,), (0,)), ((), ())), preferred_element_type=F32)
        begin = 0
        for out in outs:
            out[...] += whole[begin : begin + out.shape[0], :]
            begin += out.shape[0]
        return 0

    lax.fori_loop(0, (total + LANES - 1) // LANES, stack_up, 0)


def match(near, after, tail, parcels, sizes, dims):
    length, block = dims[-2:]
    tiles, wave_tiles = block // LANES, length // LANES
    spread = tiles + wave_tiles
    reach = (tail.shape[1] - length) // LANES
    rows = sum(parcel.shape[0] for parcel in parcels)
    wide = -(-rows // LANES) * LANES
    vmem = pl.BlockSpec(memory_space=pltpu.VMEM)
    *parts, rounds = pl.pallas_call(
        lambda *refs: match_kernel(dims, len(parcels), len(sizes), *refs),
        out_shape=[jax.ShapeDtypeStruct((size, block), F32) for size in sizes]
        + [jax.ShapeDtypeStruct((1,), jnp.int32)],
        in_specs=[vmem] * (3 + len(parcels)),
        out_specs=[vmem] * len(sizes) + [pl.BlockSpec(memory_space=pltpu.SMEM)],
        scratch_shapes=[
            pltpu.VMEM((max(2 * tiles, spread + 2 + reach) * near.shape[0], LANES), F32),
            pltpu.VMEM((wave_tiles + 1, rows, LANES), F32),
            pltpu.VMEM((wide, block), F32),
            pltpu.VMEM((wide, sum(sizes)), F32),
            pltpu.VMEM((BATCH * spread, 2 * LANES), BF16),
            pltpu.VMEM((2 * LANES, 3 * LANES), BF16),
            pltpu.VMEM((8, wide), jnp.int32),
            pltpu.SMEM((8, wide), jnp.int32),
            pltpu.SMEM((2, wide + LANES), jnp.int32),
            pltpu.SemaphoreType.DMA,
            pltpu.VMEM((BATCH * DEPTH, spread * LANES), BF16),
            pltpu.VMEM((wave_tiles * BATCH * 8, BATCH * DEPTH), BF16),
            pltpu.VMEM((BATCH, length + LANES), F32),
        ],
        compiler_params=pltpu.CompilerParams(vmem_limit_bytes=24 << 20),
        name="match",
    )(near, after, tail, *parcels)
    return parts, rounds


def serves_directly(buckets, cores):
    return buckets == 8 and cores == 2


def other_core(x):
    return lax.ppermute(x, "tm", [(0, 1), (1, 0)])


def body(samples, tail, templates, channels, moveouts, live):
    block = samples.shape[1]
    per_dev, per_slot, length = templates.shape
    slots = per_dev * per_slot
    buckets = lax.axis_size("tmpl") * lax.axis_size("chan")
    names = lax.axis_size("tmpl") * per_dev
    cores = lax.axis_size("tm")
    depth = bucket_rows(slots, buckets)
    per_owner = names // buckets
    dims = (depth, per_dev, per_owner, length, block)
    after = lax.ppermute(samples, "tm", [(i, i - 1) for i in range(1, cores)])
    direct = serves_directly(buckets, cores)
    routes = ((7, 6), (4, 5), (2, 3), (1, 0))

    def targets():
        if not direct:
            return [[jnp.int32(b) for b in range(buckets)]]
        me, core = here(), lax.axis_index("tm")
        found = [[me]]
        for first, second in routes:
            differ = jnp.where(core == 0, first, second)
            found.append([jnp.where(differ == 0, -2, me ^ differ)])
        return found

    def one_round(turn):
        sizes = [1] * (1 + len(routes)) if direct else [buckets]
        parcels = pack(turn, templates, channels, moveouts, live, sizes, targets, depth, samples.shape[0])
        if direct:
            got = []
            for parcel, differs in zip(parcels[1:], routes, strict=True):
                pairs = [
                    (c * cores + t, (c ^ differ) * cores + t)
                    for c in range(buckets)
                    for t, differ in enumerate(differs)
                    if differ
                ]
                got.append(lax.ppermute(parcel, GROUP + ("tm",), pairs))
            parcels = [parcels[0], *got, *[other_core(g) for g in got]]
        else:
            parcels = [lax.all_to_all(parcels[0], GROUP, 0, 0, tiled=True)]
        outs = [per_owner] * buckets if direct else [names]
        return match(samples, after, tail, parcels, outs, dims)

    parts, rounds = one_round(None)

    def more(state):
        return state[0] < rounds[0]

    def again(state):
        turn, values = state
        return turn + 1, [value + other for value, other in zip(values, one_round(turn)[0], strict=True)]

    _, parts = lax.while_loop(more, again, (jnp.int32(1), parts))
    if not direct:
        spread = lax.all_to_all(parts[0], GROUP, 0, 0, tiled=True)
        return jnp.sum(spread.reshape(buckets, per_owner, block), axis=0)
    result = parts[0]
    for differ in range(buckets - 1, 0, -1):
        other = lax.ppermute(parts[differ], GROUP, [(c, c ^ differ) for c in range(buckets)])
        result = result + other
    return result


def solution(mesh):
    in_specs = (
        P(("tmpl", "chan"), ("groups", "tm")),
        P(("tmpl", "chan"), "groups"),
        P("tmpl", "chan", None),
        P("tmpl", "chan"),
        P("tmpl", "chan"),
        P("tmpl"),
    )
    out_specs = P(("tmpl", "chan"), ("groups", "tm"))
    return jax.shard_map(body, mesh=mesh, in_specs=in_specs, out_specs=out_specs, check_vma=False)
```

time: 502 us -> 48.7 us (0.10)
  local copies, waits for them, and re-layouts: 271 us -> 0.69 us
  waiting for transfers between devices: 128 us -> 10.2 us
  matrix products: 71.3 us -> 0 us
  starting transfers between devices: 1.36 us -> 23.4 us
  between operations: 13.3 us -> 0.13 us
  Pallas kernels: 0 us -> 12.9 us
  other arithmetic: 11.5 us -> 0.66 us
    gather x514 -> x0, local copies, waits for them, and re-layouts: 266 us -> none
    all_gather x2 -> x0, waiting for transfers between devices: 117 us -> none  [the longest x1 64.9 us: body(): lax.all_gather(samples, ('tmpl', 'chan'), axis=0, tiled=True)]
    conv_general_dilated x1 -> x0, matrix products: 71.3 us -> none  [depthwise(): lax.conv_general_dilated(signal[None], kernel[:, None, :], (1,), 'VALID',...]
    ppermute x1 -> x16, starting transfers between devices: 1.28 us -> 23.4 us  [the longest x7 12.3 us: body(): lax.ppermute(parts[differ], GROUP, [(c, c ^ differ) for c in range(bucket...]
    pallas_call x0 -> x2, Pallas kernels: none -> 12.9 us  [the longest x1 11.4 us: match(): pl.pallas_call(lambda *refs: match_kernel(dims, len(parcels), len(sizes),...]
    ppermute x1 -> x16, waiting for transfers between devices: 0.01 us -> 10.2 us  [the longest x7 5.9 us: body(): lax.ppermute(parts[differ], GROUP, [(c, c ^ differ) for c in range(bucket...]
    reduce_scatter x1 -> x0, waiting for transfers between devices: 9.08 us -> none  [body(): lax.psum_scatter(partial_value, 'chan', scatter_dimension=0, tiled=True)]
  transfers between devices with their start and end apart: 4 -> 16, of which waited for: 3 -> 7; matrix products, arithmetic and copies ran while one was open for 2% -> 0% of each run, Pallas kernels for 0% -> 3%
where the time goes in v1:
time: 48.7 us; the launch traced here: 48.5 us
  starting transfers between devices  23.4 us (48%)
  Pallas kernels  12.9 us (26%)
  waiting for transfers between devices  10.2 us (21%)
  local copies, waits for them, and re-layouts  0.69 us (1%)
  other arithmetic  0.66 us (1%)
  loops' own time  0.61 us (1%)
    ppermute x7, starting transfers between devices, body(): lax.ppermute(parts[differ], GROUP, [(c, c ^ differ) for c in range(bucket...  12.3 us
    pallas_call x1, Pallas kernels, match(): pl.pallas_call(lambda *refs: match_kernel(dims, len(parcels), len(sizes),...  11.4 us
    ppermute x4, starting transfers between devices, one_round(): got.append(lax.ppermute(parcel, GROUP + ('tm',), pairs))  9.17 us
    ppermute x7, waiting for transfers between devices, body(): lax.ppermute(parts[differ], GROUP, [(c, c ^ differ) for c in range(bucket...  5.9 us
    ppermute x4, waiting for transfers between devices, one_round(): got.append(lax.ppermute(parcel, GROUP + ('tm',), pairs))  3.06 us
    pallas_call x1, Pallas kernels, pack(): pl.pallas_call(kernel, out_shape=[jax.ShapeDtypeStruct((size * depth, len...  1.5 us
    ppermute x1, starting transfers between devices, body(): after = lax.ppermute(samples, 'tm', [(i, i - 1) for i in range(1, cores)])  1.28 us
    ppermute x4, waiting for transfers between devices, other_core(): return lax.ppermute(x, 'tm', [(0, 1), (1, 0)])  1.23 us
  transfers between devices with their start and end apart: 16, of which 7 were waited for; matrix products, arithmetic and copies ran while one was open for 0% of the time, Pallas kernels for 3%

profile of v1, /device:TPU:0, one launch (start us, length us, event | category | flops | bytes accessed | tf_op | source)
XLA Modules:
  0.0 48.5 jit_solution(12435144878475175270)
XLA Ops:
  0.0 1.3 %collective-permute-start.8 = (bf16[224,896]{1,0:T(8,128)(2,1)}, bf16[224,896]{1,0:T(8,128)(2,1)S(1)}, u32[]{:S(2)}, u32[]{:S(2)}) collective-permute-start(bf16[224,896]{1,0:T(8,128)(2,1)} %refs_0_.3), channel_id=1, source_target_pairs={{1,0},{3,2},{5,4},{7,6},{9,8},{11,10},{13,12},{15,14},{17,16},{19,... | collective-permute-start | bytes 1204232 | tf_op jit(solution)/shard_map/ppermute | solution.py:395
  1.3 0.0 copy-start.4
  1.3 0.0 copy-start.3
  1.3 0.0 copy-start.5
  1.3 0.7 %copy-done.4 = s32[32,4]{0,1:T(4,128)S(1)} copy-done((s32[32,4]{0,1:T(4,128)S(1)}, s32[32,4]{0,1:T(4,128)}, u32[]{:S(2)}) %copy-start.4) | copy-done | bytes 536
  2.0 0.0 copy-done.3
  2.0 0.0 copy-done.5
  2.0 1.5 %pack.2 = (bf16[32,768]{1,0:T(8,128)(2,1)S(1)}, bf16[32,768]{1,0:T(8,128)(2,1)S(1)}, bf16[32,768]{1,0:T(8,128)(2,1)S(1)}, bf16[32,768]{1,0:T(8,128)(2,1)S(1)}, bf16[32,768]{1,0:T(8,128)(2,1)S(1)}) custom-call(bf16[32,4,640]{2,1,0:T(4,128)(2,1)} %refs_0_.2, s32[4,32]{1,0:T(4,128)S(1)} %bitcast.17, s32[4,32]{1,0:T(4,128)S(1)} %bitcast.19, s32[1,32]{1,0:T(1,128)S(1)} %bitcast.21), custom_call_target="tpu_custom_call" | custom-call | tf_op jit(solution)/shard_map/pack/pallas_call | solution.py:114
  3.5 6.1 %collective-permute-start.9 = (bf16[32,768]{1,0:T(8,128)(2,1)S(1)}, bf16[32,768]{1,0:T(8,128)(2,1)S(1)}, u32[]{:S(2)}, u32[]{:S(2)}) collective-permute-start(bf16[32,768]{1,0:T(8,128)(2,1)S(1)} %get-tuple-element.128), channel_id=1, source_target_pairs={{0,14},{1,13},{2,12},{3,15},{4,10},{5,9},{6,8},{7,11},{8,6},{9,5},... | collective-permute-start | bytes 147464 | tf_op jit(solution)/shard_map/ppermute | solution.py:421
  9.6 0.0 collective-permute-start.10
  9.6 0.8 %collective-permute-start.11 = (bf16[32,768]{1,0:T(8,128)(2,1)S(1)}, bf16[32,768]{1,0:T(8,128)(2,1)S(1)}, u32[]{:S(2)}, u32[]{:S(2)}) collective-permute-start(bf16[32,768]{1,0:T(8,128)(2,1)S(1)} %get-tuple-element.130), channel_id=1, source_target_pairs={{0,4},{1,7},{2,6},{3,5},{4,0},{5,3},{6,2},{7,1},{8,12},{9,15},{10,... | collective-permute-start | bytes 147464 | tf_op jit(solution)/shard_map/ppermute | solution.py:421
  10.4 2.3 %collective-permute-start.12 = (bf16[32,768]{1,0:T(8,128)(2,1)S(1)}, bf16[32,768]{1,0:T(8,128)(2,1)S(1)}, u32[]{:S(2)}, u32[]{:S(2)}) collective-permute-start(bf16[32,768]{1,0:T(8,128)(2,1)S(1)} %get-tuple-element.131), channel_id=1, source_target_pairs={{0,2},{2,0},{4,6},{6,4},{8,10},{10,8},{12,14},{14,12},{16,18},{18,... | collective-permute-start | bytes 147464 | tf_op jit(solution)/shard_map/ppermute | solution.py:421
  12.7 0.0 collective-permute-done.9.refs_4_
  12.7 0.1 collective-permute-start.13
  12.8 2.4 %collective-permute-done.10.refs_5_ = bf16[32,768]{1,0:T(8,128)(2,1)S(1)} collective-permute-done((bf16[32,768]{1,0:T(8,128)(2,1)S(1)}, bf16[32,768]{1,0:T(8,128)(2,1)S(1)}, u32[]{:S(2)}, u32[]{:S(2)}) %collective-permute-start.10) | collective-permute-done | bytes 49184 | tf_op jit(solution)/shard_map/ppermute | solution.py:421
  15.1 0.0 collective-permute-start.14
  15.1 0.0 collective-permute-done.11.refs_6_
  15.1 0.5 %collective-permute-start.15 = (bf16[32,768]{1,0:T(8,128)(2,1)S(1)}, bf16[32,768]{1,0:T(8,128)(2,1)S(1)}, u32[]{:S(2)}, u32[]{:S(2)}) collective-permute-start(bf16[32,768]{1,0:T(8,128)(2,1)S(1)} %collective-permute-done.11.refs_6_), channel_id=1, source_target_pairs={{0,1},{1,0},{2,3},{3,2},{4,5},{5,4},{6,7},{7,6},{8,9},{9,8},{10,11... | collective-permute-start | bytes 147464 | tf_op jit(solution)/shard_map/ppermute | solution.py:382
  15.6 0.7 %collective-permute-done.12.refs_7_ = bf16[32,768]{1,0:T(8,128)(2,1)S(1)} collective-permute-done((bf16[32,768]{1,0:T(8,128)(2,1)S(1)}, bf16[32,768]{1,0:T(8,128)(2,1)S(1)}, u32[]{:S(2)}, u32[]{:S(2)}) %collective-permute-start.12) | collective-permute-done | bytes 49184 | tf_op jit(solution)/shard_map/ppermute | solution.py:421
  16.3 0.0 collective-permute-start.16
  16.3 0.0 collective-permute-done.13.refs_8_
  16.3 0.0 collective-permute-done.14.refs_9_
  16.4 0.2 collective-permute-done.15.refs_10_
  16.5 1.0 %collective-permute-done.16.refs_11_ = bf16[32,768]{1,0:T(8,128)(2,1)S(1)} collective-permute-done((bf16[32,768]{1,0:T(8,128)(2,1)S(1)}, bf16[32,768]{1,0:T(8,128)(2,1)S(1)}, u32[]{:S(2)}, u32[]{:S(2)}) %collective-permute-start.16) | collective-permute-done | bytes 49184 | tf_op jit(solution)/shard_map/ppermute | solution.py:382
  17.6 0.0 collective-permute-done.8.refs_1_
  17.6 0.0 copy-start
  17.6 0.0 copy-start.1
  17.6 0.0 copy-start.2
  17.6 11.4 %match.2 = (f32[16,896]{1,0:T(8,128)S(1)}, f32[16,896]{1,0:T(8,128)S(1)}, f32[16,896]{1,0:T(8,128)S(1)}, f32[16,896]{1,0:T(8,128)S(1)}, f32[16,896]{1,0:T(8,128)...) custom-call(bf16[224,896]{1,0:T(8,128)(2,1)} %refs_0_.3, ...), custom_call_target="tpu_custom_call" | custom-call | tf_op jit(solution)/shard_map/match/pallas_call | solution.py:350
  28.9 0.0 copy-done
  29.0 0.0 copy-done.1
  29.0 0.0 copy-done.2
  29.0 0.6 %while.24 = (s32[]{:T(128)}, f32[16,896]{1,0:T(8,128)S(1)}, f32[16,896]{1,0:T(8,128)S(1)}, f32[16,896]{1,0:T(8,128)S(1)}, f32[16,896]{1,0:T(8,128)S(1)}, /*index...) while((s32[]{:T(128)}, f32[16,896]{1,0:T(8,128)S(1)}, ...), condition=%wide.region_1.0_spmd, body=%wide.region_0.0_spmd.sunk | while | flops 114690 | bytes 2949605 | solution.py:437
  29.6 4.9 %collective-permute-start.17 = (f32[16,896]{1,0:T(8,128)S(1)}, f32[16,896]{1,0:T(8,128)S(1)}, u32[]{:S(2)}, u32[]{:S(2)}) collective-permute-start(f32[16,896]{1,0:T(8,128)S(1)} %get-tuple-element.142), channel_id=1, source_target_pairs={{0,14},{2,12},{4,10},{6,8},{8,6},{10,4},{12,2},{14,0},{1,15},{3,13... | collective-permute-start | bytes 172040 | tf_op jit(solution)/shard_map/ppermute | solution.py:443
  34.5 1.5 %collective-permute-start.23 = (f32[16,896]{1,0:T(8,128)S(1)}, f32[16,896]{1,0:T(8,128)S(1)}, u32[]{:S(2)}, u32[]{:S(2)}) collective-permute-start(f32[16,896]{1,0:T(8,128)S(1)} %get-tuple-element.148), channel_id=1, source_target_pairs={{0,2},{2,0},{4,6},{6,4},{8,10},{10,8},{12,14},{14,12},{1,3},{3,1},... | collective-permute-start | bytes 172040 | tf_op jit(solution)/shard_map/ppermute | solution.py:443
  36.0 0.0 collective-permute-start.22
  36.0 2.0 %collective-permute-start.21 = (f32[16,896]{1,0:T(8,128)S(1)}, f32[16,896]{1,0:T(8,128)S(1)}, u32[]{:S(2)}, u32[]{:S(2)}) collective-permute-start(f32[16,896]{1,0:T(8,128)S(1)} %get-tuple-element.146), channel_id=1, source_target_pairs={{0,6},{2,4},{4,2},{6,0},{8,14},{10,12},{12,10},{14,8},{1,7},{3,5},... | collective-permute-start | bytes 172040 | tf_op jit(solution)/shard_map/ppermute | solution.py:443
  38.0 0.0 collective-permute-start.20
  38.0 0.0 collective-permute-done.17
  38.0 3.8 %collective-permute-start.19 = (f32[16,896]{1,0:T(8,128)S(1)}, f32[16,896]{1,0:T(8,128)S(1)}, u32[]{:S(2)}, u32[]{:S(2)}) collective-permute-start(f32[16,896]{1,0:T(8,128)S(1)} %get-tuple-element.144), channel_id=1, source_target_pairs={{0,10},{2,8},{4,14},{6,12},{8,2},{10,0},{12,6},{14,4},{1,11},{3,9}... | collective-permute-start | bytes 172040 | tf_op jit(solution)/shard_map/ppermute | solution.py:443
  41.9 0.0 collective-permute-done.23
  41.9 0.1 collective-permute-start.18
  41.9 0.0 collective-permute-done.22
  42.0 0.0 collective-permute-done.21
  42.0 2.6 %collective-permute-done.20 = f32[16,896]{1,0:T(8,128)S(1)} collective-permute-done((f32[16,896]{1,0:T(8,128)S(1)}, f32[16,896]{1,0:T(8,128)S(1)}, u32[]{:S(2)}, u32[]{:S(2)}) %collective-permute-start.20) | collective-permute-done | bytes 57376 | tf_op jit(solution)/shard_map/ppermute | solution.py:443
  44.5 2.6 %collective-permute-done.19 = f32[16,896]{1,0:T(8,128)S(1)} collective-permute-done((f32[16,896]{1,0:T(8,128)S(1)}, f32[16,896]{1,0:T(8,128)S(1)}, u32[]{:S(2)}, u32[]{:S(2)}) %collective-permute-start.19) | collective-permute-done | bytes 57376 | tf_op jit(solution)/shard_map/ppermute | solution.py:443
  47.1 0.7 %collective-permute-done.18 = f32[16,896]{1,0:T(8,128)S(1)} collective-permute-done((f32[16,896]{1,0:T(8,128)S(1)}, f32[16,896]{1,0:T(8,128)S(1)}, u32[]{:S(2)}, u32[]{:S(2)}) %collective-permute-start.18) | collective-permute-done | bytes 57376 | tf_op jit(solution)/shard_map/ppermute | solution.py:443
  47.8 0.7 %add_add_fusion = f32[16,896]{1,0:T(8,128)} fusion(f32[16,896]{1,0:T(8,128)S(1)} %collective-permute-done.23, f32[16,896]{1,0:T(8,128)S(1)} %collective-permute-done.22, f32[16,896]{1,0:T(8,128)S(1)} %collective-permute-done.21, f32[16,896]{1,0:T(8,128)S(1)} %collective-permute-done.20, f32[16,896]{1,0:T(8,128)S(1)} %collective-permute-done.19, ...), kind=kLoop, calls=%fused_computation | loop fusion | flops 100352 | bytes 516096 | tf_op jit(solution)/shard_map/add | solution.py:444
Async XLA Ops:
  0.0 17.6 %collective-permute-start.8 = (bf16[224,896]{1,0:T(8,128)(2,1)}, bf16[224,896]{1,0:T(8,128)(2,1)S(1)}, u32[]{:S(2)}, u32[]{:S(2)}) collective-permute-start(bf16[224,896]{1,0:T(8,128)(2,1)} %refs_0_.3), channel_id=1, source_target_pairs={{1,0},{3,2},{5,4},{7,6},{9,8},{11,10},{13,12},{15,14},{17,16},{19,... | collective-permute-start | bytes 1204232 | tf_op jit(solution)/shard_map/ppermute | solution.py:395
  1.3 0.7 %copy-start.4 = (s32[32,4]{0,1:T(4,128)S(1)}, s32[32,4]{0,1:T(4,128)}, u32[]{:S(2)}) copy-start(s32[32,4]{0,1:T(4,128)} %param.12) | copy-start | bytes 1540
  1.3 0.7 %copy-start.3 = (s32[32,4]{0,1:T(4,128)S(1)}, s32[32,4]{0,1:T(4,128)}, u32[]{:S(2)}) copy-start(s32[32,4]{0,1:T(4,128)} %param.11) | copy-start | bytes 1540
  1.3 0.7 %copy-start.5 = (s32[32]{0:T(128)S(1)}, s32[32]{0:T(128)}, u32[]{:S(2)}) copy-start(s32[32]{0:T(128)} %param.13) | copy-start | bytes 388
  3.5 9.2 %collective-permute-start.9 = (bf16[32,768]{1,0:T(8,128)(2,1)S(1)}, bf16[32,768]{1,0:T(8,128)(2,1)S(1)}, u32[]{:S(2)}, u32[]{:S(2)}) collective-permute-start(bf16[32,768]{1,0:T(8,128)(2,1)S(1)} %get-tuple-element.128), channel_id=1, source_target_pairs={{0,14},{1,13},{2,12},{3,15},{4,10},{5,9},{6,8},{7,11},{8,6},{9,5},... | collective-permute-start | bytes 147464 | tf_op jit(solution)/shard_map/ppermute | solution.py:421
  9.6 5.6 %collective-permute-start.10 = (bf16[32,768]{1,0:T(8,128)(2,1)S(1)}, bf16[32,768]{1,0:T(8,128)(2,1)S(1)}, u32[]{:S(2)}, u32[]{:S(2)}) collective-permute-start(bf16[32,768]{1,0:T(8,128)(2,1)S(1)} %get-tuple-element.129), channel_id=1, source_target_pairs={{0,8},{1,11},{2,10},{3,9},{4,12},{5,15},{6,14},{7,13},{8,0},{9,3},... | collective-permute-start | bytes 147464 | tf_op jit(solution)/shard_map/ppermute | solution.py:421
  9.6 5.6 %collective-permute-start.11 = (bf16[32,768]{1,0:T(8,128)(2,1)S(1)}, bf16[32,768]{1,0:T(8,128)(2,1)S(1)}, u32[]{:S(2)}, u32[]{:S(2)}) collective-permute-start(bf16[32,768]{1,0:T(8,128)(2,1)S(1)} %get-tuple-element.130), channel_id=1, source_target_pairs={{0,4},{1,7},{2,6},{3,5},{4,0},{5,3},{6,2},{7,1},{8,12},{9,15},{10,... | collective-permute-start | bytes 147464 | tf_op jit(solution)/shard_map/ppermute | solution.py:421
  10.4 6.0 %collective-permute-start.12 = (bf16[32,768]{1,0:T(8,128)(2,1)S(1)}, bf16[32,768]{1,0:T(8,128)(2,1)S(1)}, u32[]{:S(2)}, u32[]{:S(2)}) collective-permute-start(bf16[32,768]{1,0:T(8,128)(2,1)S(1)} %get-tuple-element.131), channel_id=1, source_target_pairs={{0,2},{2,0},{4,6},{6,4},{8,10},{10,8},{12,14},{14,12},{16,18},{18,... | collective-permute-start | bytes 147464 | tf_op jit(solution)/shard_map/ppermute | solution.py:421
  12.7 3.6 %collective-permute-start.13 = (bf16[32,768]{1,0:T(8,128)(2,1)S(1)}, bf16[32,768]{1,0:T(8,128)(2,1)S(1)}, u32[]{:S(2)}, u32[]{:S(2)}) collective-permute-start(bf16[32,768]{1,0:T(8,128)(2,1)S(1)} %collective-permute-done.9.refs_4_), channel_id=1, source_target_pairs={{0,1},{1,0},{2,3},{3,2},{4,5},{5,4},{6,7},{7,6},{8,9},{9,8},{10,11... | collective-permute-start | bytes 147464 | tf_op jit(solution)/shard_map/ppermute | solution.py:382
  15.1 1.2 %collective-permute-start.14 = (bf16[32,768]{1,0:T(8,128)(2,1)S(1)}, bf16[32,768]{1,0:T(8,128)(2,1)S(1)}, u32[]{:S(2)}, u32[]{:S(2)}) collective-permute-start(bf16[32,768]{1,0:T(8,128)(2,1)S(1)} %collective-permute-done.10.refs_5_), channel_id=1, source_target_pairs={{0,1},{1,0},{2,3},{3,2},{4,5},{5,4},{6,7},{7,6},{8,9},{9,8},{10,11... | collective-permute-start | bytes 147464 | tf_op jit(solution)/shard_map/ppermute | solution.py:382
  15.1 1.4 %collective-permute-start.15 = (bf16[32,768]{1,0:T(8,128)(2,1)S(1)}, bf16[32,768]{1,0:T(8,128)(2,1)S(1)}, u32[]{:S(2)}, u32[]{:S(2)}) collective-permute-start(bf16[32,768]{1,0:T(8,128)(2,1)S(1)} %collective-permute-done.11.refs_6_), channel_id=1, source_target_pairs={{0,1},{1,0},{2,3},{3,2},{4,5},{5,4},{6,7},{7,6},{8,9},{9,8},{10,11... | collective-permute-start | bytes 147464 | tf_op jit(solution)/shard_map/ppermute | solution.py:382
  16.3 1.2 %collective-permute-start.16 = (bf16[32,768]{1,0:T(8,128)(2,1)S(1)}, bf16[32,768]{1,0:T(8,128)(2,1)S(1)}, u32[]{:S(2)}, u32[]{:S(2)}) collective-permute-start(bf16[32,768]{1,0:T(8,128)(2,1)S(1)} %collective-permute-done.12.refs_7_), channel_id=1, source_target_pairs={{0,1},{1,0},{2,3},{3,2},{4,5},{5,4},{6,7},{7,6},{8,9},{9,8},{10,11... | collective-permute-start | bytes 147464 | tf_op jit(solution)/shard_map/ppermute | solution.py:382
  17.6 11.4 %copy-start = (bf16[224,896]{1,0:T(8,128)(2,1)S(1)}, bf16[224,896]{1,0:T(8,128)(2,1)}, u32[]{:S(2)}) copy-start(bf16[224,896]{1,0:T(8,128)(2,1)} %refs_0_.3) | copy-start | bytes 1204228
  17.6 11.4 %copy-start.1 = (bf16[224,896]{1,0:T(8,128)(2,1)S(1)}, bf16[224,896]{1,0:T(8,128)(2,1)}, u32[]{:S(2)}) copy-start(bf16[224,896]{1,0:T(8,128)(2,1)} %refs_2_.1) | copy-start | bytes 1204228
  17.6 11.4 %copy-start.2 = (bf16[32,4,640]{2,1,0:T(4,128)(2,1)S(1)}, bf16[32,4,640]{2,1,0:T(4,128)(2,1)}, u32[]{:S(2)}) copy-start(bf16[32,4,640]{2,1,0:T(4,128)(2,1)} %refs_0_.2) | copy-start | bytes 491524
  29.6 8.4 %collective-permute-start.17 = (f32[16,896]{1,0:T(8,128)S(1)}, f32[16,896]{1,0:T(8,128)S(1)}, u32[]{:S(2)}, u32[]{:S(2)}) collective-permute-start(f32[16,896]{1,0:T(8,128)S(1)} %get-tuple-element.142), channel_id=1, source_target_pairs={{0,14},{2,12},{4,10},{6,8},{8,6},{10,4},{12,2},{14,0},{1,15},{3,13... | collective-permute-start | bytes 172040 | tf_op jit(solution)/shard_map/ppermute | solution.py:443
  34.5 7.3 %collective-permute-start.23 = (f32[16,896]{1,0:T(8,128)S(1)}, f32[16,896]{1,0:T(8,128)S(1)}, u32[]{:S(2)}, u32[]{:S(2)}) collective-permute-start(f32[16,896]{1,0:T(8,128)S(1)} %get-tuple-element.148), channel_id=1, source_target_pairs={{0,2},{2,0},{4,6},{6,4},{8,10},{10,8},{12,14},{14,12},{1,3},{3,1},... | collective-permute-start | bytes 172040 | tf_op jit(solution)/shard_map/ppermute | solution.py:443
  36.0 5.9 %collective-permute-start.22 = (f32[16,896]{1,0:T(8,128)S(1)}, f32[16,896]{1,0:T(8,128)S(1)}, u32[]{:S(2)}, u32[]{:S(2)}) collective-permute-start(f32[16,896]{1,0:T(8,128)S(1)} %get-tuple-element.147), channel_id=1, source_target_pairs={{0,4},{2,6},{4,0},{6,2},{8,12},{10,14},{12,8},{14,10},{1,5},{3,7},... | collective-permute-start | bytes 172040 | tf_op jit(solution)/shard_map/ppermute | solution.py:443
  36.0 5.9 %collective-permute-start.21 = (f32[16,896]{1,0:T(8,128)S(1)}, f32[16,896]{1,0:T(8,128)S(1)}, u32[]{:S(2)}, u32[]{:S(2)}) collective-permute-start(f32[16,896]{1,0:T(8,128)S(1)} %get-tuple-element.146), channel_id=1, source_target_pairs={{0,6},{2,4},{4,2},{6,0},{8,14},{10,12},{12,10},{14,8},{1,7},{3,5},... | collective-permute-start | bytes 172040 | tf_op jit(solution)/shard_map/ppermute | solution.py:443
  38.0 6.5 %collective-permute-start.20 = (f32[16,896]{1,0:T(8,128)S(1)}, f32[16,896]{1,0:T(8,128)S(1)}, u32[]{:S(2)}, u32[]{:S(2)}) collective-permute-start(f32[16,896]{1,0:T(8,128)S(1)} %get-tuple-element.145), channel_id=1, source_target_pairs={{0,8},{2,10},{4,12},{6,14},{8,0},{10,2},{12,4},{14,6},{1,9},{3,11}... | collective-permute-start | bytes 172040 | tf_op jit(solution)/shard_map/ppermute | solution.py:443
  38.0 9.1 %collective-permute-start.19 = (f32[16,896]{1,0:T(8,128)S(1)}, f32[16,896]{1,0:T(8,128)S(1)}, u32[]{:S(2)}, u32[]{:S(2)}) collective-permute-start(f32[16,896]{1,0:T(8,128)S(1)} %get-tuple-element.144), channel_id=1, source_target_pairs={{0,10},{2,8},{4,14},{6,12},{8,2},{10,0},{12,6},{14,4},{1,11},{3,9}... | collective-permute-start | bytes 172040 | tf_op jit(solution)/shard_map/ppermute | solution.py:443
  41.9 6.0 %collective-permute-start.18 = (f32[16,896]{1,0:T(8,128)S(1)}, f32[16,896]{1,0:T(8,128)S(1)}, u32[]{:S(2)}, u32[]{:S(2)}) collective-permute-start(f32[16,896]{1,0:T(8,128)S(1)} %get-tuple-element.143), channel_id=1, source_target_pairs={{0,12},{2,14},{4,8},{6,10},{8,4},{10,6},{12,0},{14,2},{1,13},{3,15... | collective-permute-start | bytes 172040 | tf_op jit(solution)/shard_map/ppermute | solution.py:443
